TPU v7x, 512 devices: a whole 4x8x8 slice. The times are simulated.
512 devices in a mesh: rows: 128 (over z, y, core), cols: 4 (over x).
Axes of the slice: x: 4, y: 8, z: 8, core: 2. Of those that a mesh axis runs over, the one named last changes fastest.
Arguments:
- hidden_panel: float32 [8192, 16384], P('cols', 'rows'), may hold values from -6 to 6
- row_signs: float32 [16384], P('rows'), may hold values from -1 to 1, as said below
- sample_rows: int32 [128, 4], P('rows'), may hold values from 0 to 16383, as said below
- sample_counts: int32 [128], replicated, may hold values from 1 to 4, as said below
- ridge_weight: float32 [], replicated, may hold values from 0.5 to 2
Outputs:
- sketch_gram: float32 [8192, 8192], P('cols', 'rows')
Inputs may be any that keep to these rules, and one draw needn't show every extreme that they name: `sample_rows`: row p holds 4 distinct row numbers of p * 128 to (p + 1) * 128 - 1 in ascending order, so the whole array ascends; only the first sample_counts[p] of them are sampled, the rest are ignored. `sample_counts`: entry p counts the live slots of block p; some block has exactly 4. `row_signs`: every entry is +1 or -1.
All inputs are finite; a program needn't handle non-finite values.
Results may differ from a plain program's by a relative error of at most 0.00008.
Values sent between devices are 32-bit elements; how exact they have to be, the bound alone decides.
A program may use at most 64 MiB of HBM per device.

v0:
```python
import math
import jax
import jax.numpy as jnp
from jax import lax
from jax.sharding import PartitionSpec as P


def swapped(value, axis, bit):
    mask = 2**bit
    pairs = [(source, source ^ mask) for source in range(lax.axis_size(axis))]
    return lax.ppermute(value, axis, pairs)


def parity_signs(common, levels):
    parity = jnp.zeros_like(common)
    for bit_level in range(levels):
        parity = parity ^ common >> bit_level & 1
    return (1 - 2 * parity).astype(jnp.float32)


def sign_table(extent):
    positions = jnp.arange(extent, dtype=jnp.int32)
    return parity_signs(positions[:, None] & positions[None, :], extent.bit_length() - 1)


def local_transform(signed):
    width, length = signed.shape
    outer_size = min(128, length)
    inner_size = length // outer_size
    blocks = signed.reshape(width, outer_size, inner_size)
    blocks = jnp.einsum(
        "cab,ea->ceb", blocks, sign_table(outer_size), precision=lax.Precision.HIGHEST
    )
    blocks = jnp.einsum(
        "ceb,fb->cef", blocks, sign_table(inner_size), precision=lax.Precision.HIGHEST
    )
    return blocks.reshape(width, length)


def body(hidden_panel, row_signs, sample_rows, sample_counts, ridge_weight):
    width, length = hidden_panel.shape
    shards = lax.axis_size("rows")
    my_shard = lax.axis_index("rows")
    levels = shards.bit_length() - 1
    factor = 1.0 / math.sqrt(length * shards)
    slot_total = sample_rows.shape[1]
    spread = local_transform(hidden_panel * row_signs[None, :])
    for bit_level in range(levels):
        partner = swapped(spread, "rows", bit_level)
        upper_half = my_shard >> bit_level & 1 == 1
        spread = jnp.where(upper_half, partner - spread, spread + partner)
    picked = jnp.take(spread, sample_rows[0] - my_shard * length, axis=1) * factor
    live_slots = lax.dynamic_index_in_dim(sample_counts, my_shard, keepdims=False)
    slot_mask = (jnp.arange(slot_total) < live_slots).astype(jnp.float32)
    sketch = picked * slot_mask[None, :]
    all_slots = lax.all_gather(sketch, "rows", axis=1, tiled=True)
    all_units = lax.all_gather(sketch, "cols", axis=0, tiled=True)
    block_units = lax.all_to_all(all_units, "rows", split_axis=0, concat_axis=1, tiled=True)
    partial_value = jnp.dot(
        all_slots,
        block_units.T,
        precision=lax.Precision.HIGHEST,
        preferred_element_type=jnp.float32,
    )
    sample_total = jnp.sum(sample_counts).astype(jnp.float32)
    row_start = lax.axis_index("cols") * width
    block_width = block_units.shape[0]
    col_start = my_shard * block_width
    diagonal = (
        (row_start + jnp.arange(width))[:, None] == (col_start + jnp.arange(block_width))[None, :]
    ).astype(jnp.float32)
    return partial_value / sample_total + ridge_weight * diagonal


def solution(mesh):
    placed = (P("cols", "rows"), P("rows"), P("rows", None), P(), P())
    return jax.shard_map(
        body, mesh=mesh, in_specs=placed, out_specs=P("cols", "rows"), check_vma=False
    )
```

profile of v0, /device:TPU:1, one launch (start us, length us, event | category | flops | bytes accessed | tf_op | source)
XLA Modules:
  0.0 380.0 jit_solution(14253344918159398699)
XLA Ops:
  6.5 2.3 convolution_bitcast_fusion
  8.8 8.8 %collective-permute-start = (f32[2048,128]{0,1:T(8,128)S(1)}, f32[2048,128]{0,1:T(8,128)S(1)}, u32[]{:S(2)}, u32[]{:S(2)}) collective-permute-start(f32[2048,128]{0,1:T(8,128)S(1)} %convolution_bitcast_fusion), channel_id=1, source_target_pairs={{0,4},{4,0},{8,12},{12,8},{16,20},{20,16},{24,28},{28,24},{32,36},... | collective-permute-start | bytes 3145736 | tf_op jit(solution)/shard_map/ppermute | solution.py:11
  17.6 2.3 collective-permute-done
  20.0 1.9 collective-permute-start.1
  22.0 24.3 %collective-permute-done.1 = f32[2048,128]{0,1:T(8,128)S(1)} collective-permute-done((f32[2048,128]{0,1:T(8,128)S(1)}, f32[2048,128]{0,1:T(8,128)S(1)}, u32[]{:S(2)}, u32[]{:S(2)}) %collective-permute-start.1) | collective-permute-done | bytes 1048608 | tf_op jit(solution)/shard_map/ppermute | solution.py:11
  46.5 1.9 collective-permute-start.2
  48.4 48.4 %collective-permute-done.2 = f32[2048,128]{0,1:T(8,128)S(1)} collective-permute-done((f32[2048,128]{0,1:T(8,128)S(1)}, f32[2048,128]{0,1:T(8,128)S(1)}, u32[]{:S(2)}, u32[]{:S(2)}) %collective-permute-start.2) | collective-permute-done | bytes 1048608 | tf_op jit(solution)/shard_map/ppermute | solution.py:11
  96.9 2.0 collective-permute-start.3
  99.0 47.9 %collective-permute-done.3 = f32[2048,128]{0,1:T(8,128)S(1)} collective-permute-done((f32[2048,128]{0,1:T(8,128)S(1)}, f32[2048,128]{0,1:T(8,128)S(1)}, u32[]{:S(2)}, u32[]{:S(2)}) %collective-permute-start.3) | collective-permute-done | bytes 1048608 | tf_op jit(solution)/shard_map/ppermute | solution.py:11
  147.0 1.9 collective-permute-start.4
  148.9 23.2 %collective-permute-done.4 = f32[2048,128]{0,1:T(8,128)S(1)} collective-permute-done((f32[2048,128]{0,1:T(8,128)S(1)}, f32[2048,128]{0,1:T(8,128)S(1)}, u32[]{:S(2)}, u32[]{:S(2)}) %collective-permute-start.4) | collective-permute-done | bytes 1048608 | tf_op jit(solution)/shard_map/ppermute | solution.py:11
  172.2 4.7 %collective-permute-start.5 = (f32[2048,128]{0,1:T(8,128)S(1)}, f32[2048,128]{0,1:T(8,128)S(1)}, u32[]{:S(2)}, u32[]{:S(2)}) collective-permute-start(f32[2048,128]{0,1:T(8,128)S(1)} %add_select_fusion.2), channel_id=1, source_target_pairs={{0,128},{4,132},{8,136},{12,140},{16,144},{20,148},{24,152},{28,15... | collective-permute-start | bytes 3145736 | tf_op jit(solution)/shard_map/ppermute | solution.py:11
  176.9 45.1 %collective-permute-done.5 = f32[2048,128]{0,1:T(8,128)S(1)} collective-permute-done((f32[2048,128]{0,1:T(8,128)S(1)}, f32[2048,128]{0,1:T(8,128)S(1)}, u32[]{:S(2)}, u32[]{:S(2)}) %collective-permute-start.5) | collective-permute-done | bytes 1048608 | tf_op jit(solution)/shard_map/ppermute | solution.py:11
  222.2 8.2 %collective-permute-start.6 = (f32[2048,128]{0,1:T(8,128)S(1)}, f32[2048,128]{0,1:T(8,128)S(1)}, u32[]{:S(2)}, u32[]{:S(2)}) collective-permute-start(f32[2048,128]{0,1:T(8,128)S(1)} %add_select_fusion.1), channel_id=1, source_target_pairs={{0,256},{4,260},{8,264},{12,268},{16,272},{20,276},{24,280},{28,28... | collective-permute-start | bytes 3145736 | tf_op jit(solution)/shard_map/ppermute | solution.py:11
  230.3 0.6 dynamic_slice.4
  230.9 0.6 compare_select_fusion.2
  231.6 43.6 %collective-permute-done.6 = f32[2048,128]{0,1:T(8,128)S(1)} collective-permute-done((f32[2048,128]{0,1:T(8,128)S(1)}, f32[2048,128]{0,1:T(8,128)S(1)}, u32[]{:S(2)}, u32[]{:S(2)}) %collective-permute-start.6) | collective-permute-done | bytes 1048608 | tf_op jit(solution)/shard_map/ppermute | solution.py:11
  275.4 0.6 gather_fusion
  275.9 0.7 fusion.37
  276.6 9.5 %all_gather.7 = f32[8192,4]{0,1:T(4,128)S(1)} all-gather(f32[2048,4]{0,1:T(4,128)S(1)} %get-tuple-element.5), channel_id=1, replica_groups=mesh['rows'=128,'cols'=4] {'cols'}, dimensions={0}, use_global_device_ids=true | all-gather | bytes 163840 | tf_op jit(solution)/shard_map/all_gather | solution.py:57
  286.1 0.2 all_to_all.14
  286.3 0.2 copy.9
  286.5 0.9 reshape.65
  287.4 15.0 %all-to-all-start = ((f32[128,1,256]{2,1,0:T(1,128)}), f32[128,1,256]{2,1,0:T(1,128)S(1)}, u32[]{:S(2)}, u32[]{:S(2)}) async-start(f32[128,1,256]{2,1,0:T(1,128)} %reshape.65), calls=%async_computation | async-start | bytes 262144 | tf_op jit(solution)/shard_map/all_to_all | solution.py:58
  302.4 0.6 reduce_sum.9
  304.3 11.1 %all-to-all-done = f32[128,1,256]{2,1,0:T(1,128)S(1)} async-done(((f32[128,1,256]{2,1,0:T(1,128)}), f32[128,1,256]{2,1,0:T(1,128)S(1)}, u32[]{:S(2)}, u32[]{:S(2)}) %all-to-all-start) | async-done | bytes 131104 | tf_op jit(solution)/shard_map/all_to_all | solution.py:58
  315.4 0.5 broadcast.102
  315.9 1.0 reduce
  316.9 0.2 reshape.66
  317.0 45.1 %all-gather.3.cloned.1.call-done = f32[128,4,2048]{2,1,0:T(4,128)} async-done(((f32[1,4,2048]{2,1,0:T(4,128)}), f32[128,4,2048]{2,1,0:T(4,128)}) %all-gather.3.cloned.1.call-update) | async-done | bytes 4194320 | tf_op jit(solution)/shard_map/all_gather | solution.py:56
  362.1 5.3 %reshape.64 = f32[512,2048]{1,0:T(8,128)} reshape(f32[128,4,2048]{2,1,0:T(4,128)} %all-gather.3.cloned.1.call-done) | data formatting | bytes 8388608
  367.4 5.8 %fusion = f32[2048,64]{0,1:T(8,128)} fusion(f32[512,2048]{1,0:T(8,128)} %reshape.64, f32[64,512]{0,1:T(8,128)S(1)} %bitcast.28, f32[]{:T(128)S(6)} %copy.10, s32[2048]{0:T(1024)S(1)} %iota_add_fusion, f32[]{:T(128)S(6)} %convert_element_type.13, s32[64]{0:T(128)S(1)} %iota_add_fusion.1), kind=kOutput, calls=%fused_computation.3 | convolution fusion | flops 805830656 | bytes 4858120 | tf_op jit(solution)/shard_map/dot_general | solution.py:59
  (18 shorter events, 1.1 us)
Async XLA Ops:
  6.5 355.6 %all-gather.3.cloned.1.call-start = ((), (), s32[]{:S(2)}) async-start(), calls=%async_computation.1 | async-start | bytes 4227072 | tf_op jit(solution)/shard_map/all_gather | solution.py:56
  8.8 11.1 %collective-permute-start = (f32[2048,128]{0,1:T(8,128)S(1)}, f32[2048,128]{0,1:T(8,128)S(1)}, u32[]{:S(2)}, u32[]{:S(2)}) collective-permute-start(f32[2048,128]{0,1:T(8,128)S(1)} %convolution_bitcast_fusion), channel_id=1, source_target_pairs={{0,4},{4,0},{8,12},{12,8},{16,20},{20,16},{24,28},{28,24},{32,36},... | collective-permute-start | bytes 3145736 | tf_op jit(solution)/shard_map/ppermute | solution.py:11
  20.0 26.3 %collective-permute-start.1 = (f32[2048,128]{0,1:T(8,128)S(1)}, f32[2048,128]{0,1:T(8,128)S(1)}, u32[]{:S(2)}, u32[]{:S(2)}) collective-permute-start(f32[2048,128]{0,1:T(8,128)S(1)} %add_select_fusion.6), channel_id=1, source_target_pairs={{0,8},{4,12},{8,0},{12,4},{16,24},{20,28},{24,16},{28,20},{32,40},... | collective-permute-start | bytes 3145736 | tf_op jit(solution)/shard_map/ppermute | solution.py:11
  46.5 50.3 %collective-permute-start.2 = (f32[2048,128]{0,1:T(8,128)S(1)}, f32[2048,128]{0,1:T(8,128)S(1)}, u32[]{:S(2)}, u32[]{:S(2)}) collective-permute-start(f32[2048,128]{0,1:T(8,128)S(1)} %add_select_fusion.5), channel_id=1, source_target_pairs={{0,16},{4,20},{8,24},{12,28},{16,0},{20,4},{24,8},{28,12},{32,48},... | collective-permute-start | bytes 3145736 | tf_op jit(solution)/shard_map/ppermute | solution.py:11
  96.9 49.9 %collective-permute-start.3 = (f32[2048,128]{0,1:T(8,128)S(1)}, f32[2048,128]{0,1:T(8,128)S(1)}, u32[]{:S(2)}, u32[]{:S(2)}) collective-permute-start(f32[2048,128]{0,1:T(8,128)S(1)} %add_select_fusion.4), channel_id=1, source_target_pairs={{0,32},{4,36},{8,40},{12,44},{16,48},{20,52},{24,56},{28,60},{32,0... | collective-permute-start | bytes 3145736 | tf_op jit(solution)/shard_map/ppermute | solution.py:11
  98.9 131.4 %copy-start.1 = (s32[128]{0:T(128)S(1)}, s32[128]{0:T(128)}, u32[]{:S(2)}) copy-start(s32[128]{0:T(128)} %param.8) | copy-start | bytes 1540
  98.9 132.7 %copy-start = (s32[1,4]{1,0:T(1,128)S(1)}, s32[1,4]{1,0:T(1,128)}, u32[]{:S(2)}) copy-start(s32[1,4]{1,0:T(1,128)} %param.7) | copy-start | bytes 52
  147.0 25.1 %collective-permute-start.4 = (f32[2048,128]{0,1:T(8,128)S(1)}, f32[2048,128]{0,1:T(8,128)S(1)}, u32[]{:S(2)}, u32[]{:S(2)}) collective-permute-start(f32[2048,128]{0,1:T(8,128)S(1)} %add_select_fusion.3), channel_id=1, source_target_pairs={{0,64},{4,68},{8,72},{12,76},{16,80},{20,84},{24,88},{28,92},{32,9... | collective-permute-start | bytes 3145736 | tf_op jit(solution)/shard_map/ppermute | solution.py:11
  172.2 49.8 %collective-permute-start.5 = (f32[2048,128]{0,1:T(8,128)S(1)}, f32[2048,128]{0,1:T(8,128)S(1)}, u32[]{:S(2)}, u32[]{:S(2)}) collective-permute-start(f32[2048,128]{0,1:T(8,128)S(1)} %add_select_fusion.2), channel_id=1, source_target_pairs={{0,128},{4,132},{8,136},{12,140},{16,144},{20,148},{24,152},{28,15... | collective-permute-start | bytes 3145736 | tf_op jit(solution)/shard_map/ppermute | solution.py:11
  222.2 53.0 %collective-permute-start.6 = (f32[2048,128]{0,1:T(8,128)S(1)}, f32[2048,128]{0,1:T(8,128)S(1)}, u32[]{:S(2)}, u32[]{:S(2)}) collective-permute-start(f32[2048,128]{0,1:T(8,128)S(1)} %add_select_fusion.1), channel_id=1, source_target_pairs={{0,256},{4,260},{8,264},{12,268},{16,272},{20,276},{24,280},{28,28... | collective-permute-start | bytes 3145736 | tf_op jit(solution)/shard_map/ppermute | solution.py:11
  287.4 28.0 %all-to-all-start = ((f32[128,1,256]{2,1,0:T(1,128)}), f32[128,1,256]{2,1,0:T(1,128)S(1)}, u32[]{:S(2)}, u32[]{:S(2)}) async-start(f32[128,1,256]{2,1,0:T(1,128)} %reshape.65), calls=%async_computation | async-start | bytes 262144 | tf_op jit(solution)/shard_map/all_to_all | solution.py:58
Sparse Core Ops, SparseCore 0:
  276.8 85.2 all-gather.2
where the time goes:
time: 381 us; the launch traced here: 380 us
  waiting for transfers between devices  291 us (76%)
  starting transfers between devices  44.5 us (12%)
  between operations  14.9 us (4%)
  blocking collectives  9.46 us (2%)
  local copies, waits for them, and re-layouts  8.41 us (2%)
  matrix products  8.04 us (2%)
  other arithmetic  3.98 us (1%)
    ppermute x7, waiting for transfers between devices, swapped(): return lax.ppermute(value, axis, pairs)  235 us
    all_gather x1, waiting for transfers between devices, body(): all_slots = lax.all_gather(sketch, 'rows', axis=1, tiled=True)  45.1 us
    ppermute x7, starting transfers between devices, swapped(): return lax.ppermute(value, axis, pairs)  29.4 us
    all_to_all x1, starting transfers between devices, body(): lax.all_to_all(all_units, 'rows', split_axis=0, concat_axis=1, tiled=True)  15 us
    all_to_all x1, waiting for transfers between devices, body(): lax.all_to_all(all_units, 'rows', split_axis=0, concat_axis=1, tiled=True)  11.1 us
    all_gather x1, blocking collectives, body(): all_units = lax.all_gather(sketch, 'cols', axis=0, tiled=True)  9.46 us
  transfers between devices with their start and end apart: 9, of which 9 were waited for; matrix products, arithmetic and copies ran while one was open for 1% of the time, Pallas kernels for 0%

commit v1 on v0

--- a/solution.py
+++ b/solution.py
@@ -3,6 +3,7 @@
 import jax.numpy as jnp
 from jax import lax
 from jax.sharding import PartitionSpec as P
+from jax.lax import all_to_all, axis_size
 
 
 def swapped(value, axis, bit):
@@ -55,7 +56,9 @@
     sketch = picked * slot_mask[None, :]
     all_slots = lax.all_gather(sketch, "rows", axis=1, tiled=True)
     all_units = lax.all_gather(sketch, "cols", axis=0, tiled=True)
-    block_units = lax.all_to_all(all_units, "rows", split_axis=0, concat_axis=1, tiled=True)
+    block_units = jnp.concatenate(
+        all_to_all(jnp.stack(jnp.split(all_units, axis_size("rows"), axis=0)), "rows", 0, 0), axis=1
+    )
     partial_value = jnp.dot(
         all_slots,
         block_units.T,

time: 381 us -> 381 us (level)
  local copies, waits for them, and re-layouts: 8.41 us -> 13.5 us
  waiting for transfers between devices: 291 us -> 286 us
    unnamed x7 -> x134, local copies, waits for them, and re-layouts: 6.38 us -> 11.7 us
    all_gather x1, waiting for transfers between devices: 45.1 us -> 40.7 us  [body(): all_slots = lax.all_gather(sketch, 'rows', axis=1, tiled=True)]
  transfers between devices with their start and end apart: 9 -> 9, of which waited for: 9 -> 9; matrix products, arithmetic and copies ran while one was open for 1% -> 3% of each run, Pallas kernels for 0% -> 0%
where the time goes in v1:
time: 381 us; the launch traced here: 380 us
  waiting for transfers between devices  286 us (75%)
  starting transfers between devices  44.5 us (12%)
  between operations  14.9 us (4%)
  local copies, waits for them, and re-layouts  13.5 us (4%)
  blocking collectives  9.46 us (2%)
  matrix products  8.04 us (2%)
  other arithmetic  3.98 us (1%)
    ppermute x7, waiting for transfers between devices, swapped(): return lax.ppermute(value, axis, pairs)  235 us
    all_gather x1, waiting for transfers between devices, body(): all_slots = lax.all_gather(sketch, 'rows', axis=1, tiled=True)  40.7 us
    ppermute x7, starting transfers between devices, swapped(): return lax.ppermute(value, axis, pairs)  29.4 us
    all_to_all x1, starting transfers between devices, body(): all_to_all(jnp.stack(jnp.split(all_units, axis_size('rows'), axis=0)), 'r...  15 us
    unnamed x134, local copies, waits for them, and re-layouts  11.7 us
    all_to_all x1, waiting for transfers between devices, body(): all_to_all(jnp.stack(jnp.split(all_units, axis_size('rows'), axis=0)), 'r...  10.8 us
    all_gather x1, blocking collectives, body(): all_units = lax.all_gather(sketch, 'cols', axis=0, tiled=True)  9.46 us
  transfers between devices with their start and end apart: 9, of which 9 were waited for; matrix products, arithmetic and copies ran while one was open for 3% of the time, Pallas kernels for 0%

profile of v1, /device:TPU:1, one launch (start us, length us, event | category | flops | bytes accessed | tf_op | source)
XLA Modules:
  0.0 380.5 jit_solution(3538021883850363221)
XLA Ops:
  6.5 2.3 convolution_bitcast_fusion
  8.8 8.8 %collective-permute-start = (f32[2048,128]{0,1:T(8,128)S(1)}, f32[2048,128]{0,1:T(8,128)S(1)}, u32[]{:S(2)}, u32[]{:S(2)}) collective-permute-start(f32[2048,128]{0,1:T(8,128)S(1)} %convolution_bitcast_fusion), channel_id=1, source_target_pairs={{0,4},{4,0},{8,12},{12,8},{16,20},{20,16},{24,28},{28,24},{32,36},... | collective-permute-start | bytes 3145736 | tf_op jit(solution)/shard_map/ppermute | solution.py:12
  17.6 2.3 collective-permute-done
  20.0 1.9 collective-permute-start.1
  22.0 24.3 %collective-permute-done.1 = f32[2048,128]{0,1:T(8,128)S(1)} collective-permute-done((f32[2048,128]{0,1:T(8,128)S(1)}, f32[2048,128]{0,1:T(8,128)S(1)}, u32[]{:S(2)}, u32[]{:S(2)}) %collective-permute-start.1) | collective-permute-done | bytes 1048608 | tf_op jit(solution)/shard_map/ppermute | solution.py:12
  46.5 1.9 collective-permute-start.2
  48.4 48.4 %collective-permute-done.2 = f32[2048,128]{0,1:T(8,128)S(1)} collective-permute-done((f32[2048,128]{0,1:T(8,128)S(1)}, f32[2048,128]{0,1:T(8,128)S(1)}, u32[]{:S(2)}, u32[]{:S(2)}) %collective-permute-start.2) | collective-permute-done | bytes 1048608 | tf_op jit(solution)/shard_map/ppermute | solution.py:12
  96.7 0.1 add_select_fusion.4
  96.9 2.0 collective-permute-start.3
  99.0 47.9 %collective-permute-done.3 = f32[2048,128]{0,1:T(8,128)S(1)} collective-permute-done((f32[2048,128]{0,1:T(8,128)S(1)}, f32[2048,128]{0,1:T(8,128)S(1)}, u32[]{:S(2)}, u32[]{:S(2)}) %collective-permute-start.3) | collective-permute-done | bytes 1048608 | tf_op jit(solution)/shard_map/ppermute | solution.py:12
  147.0 1.9 collective-permute-start.4
  148.9 23.2 %collective-permute-done.4 = f32[2048,128]{0,1:T(8,128)S(1)} collective-permute-done((f32[2048,128]{0,1:T(8,128)S(1)}, f32[2048,128]{0,1:T(8,128)S(1)}, u32[]{:S(2)}, u32[]{:S(2)}) %collective-permute-start.4) | collective-permute-done | bytes 1048608 | tf_op jit(solution)/shard_map/ppermute | solution.py:12
  172.1 0.1 add_select_fusion.2
  172.2 4.7 %collective-permute-start.5 = (f32[2048,128]{0,1:T(8,128)S(1)}, f32[2048,128]{0,1:T(8,128)S(1)}, u32[]{:S(2)}, u32[]{:S(2)}) collective-permute-start(f32[2048,128]{0,1:T(8,128)S(1)} %add_select_fusion.2), channel_id=1, source_target_pairs={{0,128},{4,132},{8,136},{12,140},{16,144},{20,148},{24,152},{28,15... | collective-permute-start | bytes 3145736 | tf_op jit(solution)/shard_map/ppermute | solution.py:12
  176.9 45.1 %collective-permute-done.5 = f32[2048,128]{0,1:T(8,128)S(1)} collective-permute-done((f32[2048,128]{0,1:T(8,128)S(1)}, f32[2048,128]{0,1:T(8,128)S(1)}, u32[]{:S(2)}, u32[]{:S(2)}) %collective-permute-start.5) | collective-permute-done | bytes 1048608 | tf_op jit(solution)/shard_map/ppermute | solution.py:12
  222.2 8.2 %collective-permute-start.6 = (f32[2048,128]{0,1:T(8,128)S(1)}, f32[2048,128]{0,1:T(8,128)S(1)}, u32[]{:S(2)}, u32[]{:S(2)}) collective-permute-start(f32[2048,128]{0,1:T(8,128)S(1)} %add_select_fusion.1), channel_id=1, source_target_pairs={{0,256},{4,260},{8,264},{12,268},{16,272},{20,276},{24,280},{28,28... | collective-permute-start | bytes 3145736 | tf_op jit(solution)/shard_map/ppermute | solution.py:12
  230.3 0.6 dynamic_slice.4
  230.9 0.6 compare_select_fusion.2
  231.6 43.6 %collective-permute-done.6 = f32[2048,128]{0,1:T(8,128)S(1)} collective-permute-done((f32[2048,128]{0,1:T(8,128)S(1)}, f32[2048,128]{0,1:T(8,128)S(1)}, u32[]{:S(2)}, u32[]{:S(2)}) %collective-permute-start.6) | collective-permute-done | bytes 1048608 | tf_op jit(solution)/shard_map/ppermute | solution.py:12
  275.4 0.6 gather_fusion
  275.9 0.7 fusion.37
  276.6 9.5 %all_gather.7 = f32[8192,4]{0,1:T(4,128)S(1)} all-gather(f32[2048,4]{0,1:T(4,128)S(1)} %get-tuple-element.5), channel_id=1, replica_groups=mesh['rows'=128,'cols'=4] {'cols'}, dimensions={0}, use_global_device_ids=true | all-gather | bytes 163840 | tf_op jit(solution)/shard_map/all_gather | solution.py:58
  291.6 0.9 reshape.70
  292.5 15.0 %all-to-all-start = ((f32[128,1,256]{2,1,0:T(1,128)}), f32[128,1,256]{2,1,0:T(1,128)S(1)}, u32[]{:S(2)}, u32[]{:S(2)}) async-start(f32[128,1,256]{2,1,0:T(1,128)} %reshape.70), calls=%async_computation | async-start | bytes 262144 | tf_op jit(solution)/shard_map/all_to_all | solution.py:60
  307.5 0.6 reduce_sum.9
  309.4 10.8 %all-to-all-done = f32[128,1,256]{2,1,0:T(1,128)S(1)} async-done(((f32[128,1,256]{2,1,0:T(1,128)}), f32[128,1,256]{2,1,0:T(1,128)S(1)}, u32[]{:S(2)}, u32[]{:S(2)}) %all-to-all-start) | async-done | bytes 131104 | tf_op jit(solution)/shard_map/all_to_all | solution.py:60
  320.2 0.5 broadcast.102
  320.7 1.0 reduce
  321.7 0.2 reshape.71
  321.8 40.7 %all-gather.3.cloned.1.call-done = f32[128,4,2048]{2,1,0:T(4,128)} async-done(((f32[1,4,2048]{2,1,0:T(4,128)}), f32[128,4,2048]{2,1,0:T(4,128)}) %all-gather.3.cloned.1.call-update) | async-done | bytes 4194320 | tf_op jit(solution)/shard_map/all_gather | solution.py:57
  362.6 5.3 %reshape.69 = f32[512,2048]{1,0:T(8,128)} reshape(f32[128,4,2048]{2,1,0:T(4,128)} %all-gather.3.cloned.1.call-done) | data formatting | bytes 8388608
  367.9 5.8 %fusion = f32[2048,64]{0,1:T(8,128)} fusion(f32[512,2048]{1,0:T(8,128)} %reshape.69, f32[64,512]{0,1:T(8,128)S(1)} %bitcast.536, f32[]{:T(128)S(6)} %copy.133, s32[2048]{0:T(1024)S(1)} %iota_add_fusion, f32[]{:T(128)S(6)} %convert_element_type.13, s32[64]{0:T(128)S(1)} %iota_add_fusion.1), kind=kOutput, calls=%fused_computation.3 | convolution fusion | flops 805830656 | bytes 4858120 | tf_op jit(solution)/shard_map/dot_general | solution.py:62
  (144 shorter events, 6.2 us)
Async XLA Ops:
  6.5 356.0 %all-gather.3.cloned.1.call-start = ((), (), s32[]{:S(2)}) async-start(), calls=%async_computation.1 | async-start | bytes 4227072 | tf_op jit(solution)/shard_map/all_gather | solution.py:57
  8.8 11.1 %collective-permute-start = (f32[2048,128]{0,1:T(8,128)S(1)}, f32[2048,128]{0,1:T(8,128)S(1)}, u32[]{:S(2)}, u32[]{:S(2)}) collective-permute-start(f32[2048,128]{0,1:T(8,128)S(1)} %convolution_bitcast_fusion), channel_id=1, source_target_pairs={{0,4},{4,0},{8,12},{12,8},{16,20},{20,16},{24,28},{28,24},{32,36},... | collective-permute-start | bytes 3145736 | tf_op jit(solution)/shard_map/ppermute | solution.py:12
  20.0 26.3 %collective-permute-start.1 = (f32[2048,128]{0,1:T(8,128)S(1)}, f32[2048,128]{0,1:T(8,128)S(1)}, u32[]{:S(2)}, u32[]{:S(2)}) collective-permute-start(f32[2048,128]{0,1:T(8,128)S(1)} %add_select_fusion.6), channel_id=1, source_target_pairs={{0,8},{4,12},{8,0},{12,4},{16,24},{20,28},{24,16},{28,20},{32,40},... | collective-permute-start | bytes 3145736 | tf_op jit(solution)/shard_map/ppermute | solution.py:12
  46.5 50.3 %collective-permute-start.2 = (f32[2048,128]{0,1:T(8,128)S(1)}, f32[2048,128]{0,1:T(8,128)S(1)}, u32[]{:S(2)}, u32[]{:S(2)}) collective-permute-start(f32[2048,128]{0,1:T(8,128)S(1)} %add_select_fusion.5), channel_id=1, source_target_pairs={{0,16},{4,20},{8,24},{12,28},{16,0},{20,4},{24,8},{28,12},{32,48},... | collective-permute-start | bytes 3145736 | tf_op jit(solution)/shard_map/ppermute | solution.py:12
  96.9 49.9 %collective-permute-start.3 = (f32[2048,128]{0,1:T(8,128)S(1)}, f32[2048,128]{0,1:T(8,128)S(1)}, u32[]{:S(2)}, u32[]{:S(2)}) collective-permute-start(f32[2048,128]{0,1:T(8,128)S(1)} %add_select_fusion.4), channel_id=1, source_target_pairs={{0,32},{4,36},{8,40},{12,44},{16,48},{20,52},{24,56},{28,60},{32,0... | collective-permute-start | bytes 3145736 | tf_op jit(solution)/shard_map/ppermute | solution.py:12
  98.9 131.4 %copy-start.1 = (s32[128]{0:T(128)S(1)}, s32[128]{0:T(128)}, u32[]{:S(2)}) copy-start(s32[128]{0:T(128)} %param.8) | copy-start | bytes 1540
  98.9 132.7 %copy-start = (s32[1,4]{1,0:T(1,128)S(1)}, s32[1,4]{1,0:T(1,128)}, u32[]{:S(2)}) copy-start(s32[1,4]{1,0:T(1,128)} %param.7) | copy-start | bytes 52
  147.0 25.1 %collective-permute-start.4 = (f32[2048,128]{0,1:T(8,128)S(1)}, f32[2048,128]{0,1:T(8,128)S(1)}, u32[]{:S(2)}, u32[]{:S(2)}) collective-permute-start(f32[2048,128]{0,1:T(8,128)S(1)} %add_select_fusion.3), channel_id=1, source_target_pairs={{0,64},{4,68},{8,72},{12,76},{16,80},{20,84},{24,88},{28,92},{32,9... | collective-permute-start | bytes 3145736 | tf_op jit(solution)/shard_map/ppermute | solution.py:12
  172.2 49.8 %collective-permute-start.5 = (f32[2048,128]{0,1:T(8,128)S(1)}, f32[2048,128]{0,1:T(8,128)S(1)}, u32[]{:S(2)}, u32[]{:S(2)}) collective-permute-start(f32[2048,128]{0,1:T(8,128)S(1)} %add_select_fusion.2), channel_id=1, source_target_pairs={{0,128},{4,132},{8,136},{12,140},{16,144},{20,148},{24,152},{28,15... | collective-permute-start | bytes 3145736 | tf_op jit(solution)/shard_map/ppermute | solution.py:12
  222.2 53.0 %collective-permute-start.6 = (f32[2048,128]{0,1:T(8,128)S(1)}, f32[2048,128]{0,1:T(8,128)S(1)}, u32[]{:S(2)}, u32[]{:S(2)}) collective-permute-start(f32[2048,128]{0,1:T(8,128)S(1)} %add_select_fusion.1), channel_id=1, source_target_pairs={{0,256},{4,260},{8,264},{12,268},{16,272},{20,276},{24,280},{28,28... | collective-permute-start | bytes 3145736 | tf_op jit(solution)/shard_map/ppermute | solution.py:12
  292.5 27.7 %all-to-all-start = ((f32[128,1,256]{2,1,0:T(1,128)}), f32[128,1,256]{2,1,0:T(1,128)S(1)}, u32[]{:S(2)}, u32[]{:S(2)}) async-start(f32[128,1,256]{2,1,0:T(1,128)} %reshape.70), calls=%async_computation | async-start | bytes 262144 | tf_op jit(solution)/shard_map/all_to_all | solution.py:60
Sparse Core Ops, SparseCore 0:
  276.8 85.7 all-gather.2
